TPU v7x, 32 devices: a whole 2x2x4 slice. The times are simulated.
32 devices in a mesh: bas: 8 (over y, x, core), aux: 4 (over z).
Axes of the slice: x: 2, y: 2, z: 4, core: 2. Of those that a mesh axis runs over, the one named last changes fastest.
Arguments:
- integrals: bfloat16 [4, 8192, 8192], P('aux', 'bas'), may hold values from -6 to 6
- screen: int32 [4, 64, 64], P('aux', 'bas'), may hold values from 0 to 1, as said below
- coefficients: bfloat16 [8192, 384], P('bas'), may hold values from -0.0625 to 0.0625
- weights: float32 [384], replicated, may hold values from -2 to 2
Outputs:
- exchange: bfloat16 [8192, 8192], P('aux', 'bas')
Inputs may be any that keep to these rules, and one draw needn't show every extreme that they name: `screen`: every block with equal row and column block index is 1; the share of ones differs from row block to row block.
All inputs are finite; a program needn't handle non-finite values.
Results may differ from a plain program's by a relative error of at most 0.018.
Values may be sent and summed in bfloat16 or wider, within the bound.
A program may use at most 128 MiB of HBM per device.

v0:
```python
import math
import jax
import jax.numpy as jnp
from jax import lax
from jax.sharding import PartitionSpec as P

NOCC = 384
BLOCK = 128
AUX_DEV = 1


def spread_2(block, axis, owner):
    block = jnp.where(lax.axis_index(axis) == owner, block, jnp.zeros_like(block))
    return lax.psum(block, axis)


def shards(integrals, screen, coefficients, weights):
    aux_count = integrals.shape[0]
    row_count = integrals.shape[1]
    basis_count = integrals.shape[2]
    occ_count = coefficients.shape[1]
    row_blocks = row_count // BLOCK
    col_blocks = basis_count // BLOCK
    masks = screen.reshape(aux_count, row_blocks, 1, col_blocks, 1).astype(jnp.bfloat16)
    masked = integrals.reshape(aux_count, row_blocks, BLOCK, col_blocks, BLOCK) * masks
    flat = masked.reshape(aux_count * row_count, basis_count)
    summed_half = jnp.dot(
        flat,
        lax.all_gather(coefficients, "bas", axis=0, tiled=True),
        preferred_element_type=jnp.float32,
    )
    half = summed_half.reshape(aux_count, row_count, occ_count).transpose(1, 0, 2)
    half = half.reshape(row_count, aux_count * occ_count).astype(jnp.bfloat16)
    aux_groups = lax.axis_size("aux")
    scale = 1.0 / math.sqrt(AUX_DEV * aux_groups * NOCC)
    every = lax.all_gather(half, "aux", axis=1, tiled=True)
    weighted_all = (every.astype(jnp.float32) * jnp.tile(weights, aux_count * aux_groups)).astype(
        jnp.bfloat16
    )
    spread = lax.axis_size("bas") // aux_groups
    first = lax.axis_index("aux") * spread
    received = [spread_2(every, "bas", first + offset) for offset in range(spread)]
    owned = jnp.concatenate(received, axis=0)
    per_group = aux_count * occ_count
    left = owned.reshape(owned.shape[0], aux_groups, per_group)
    right = weighted_all.reshape(row_count, aux_groups, per_group)
    terms = jnp.einsum("ngk,mgk->gnm", left, right, preferred_element_type=jnp.float32)
    rounded = lax.optimization_barrier(terms.astype(jnp.bfloat16))
    total = jnp.sum(rounded.astype(jnp.float32), axis=0)
    return (total * scale).astype(jnp.bfloat16)


def solution(mesh):
    in_specs = (P("aux", "bas", None), P("aux", "bas", None), P("bas", None), P())
    out_specs = P("aux", "bas")
    return jax.shard_map(shards, mesh=mesh, in_specs=in_specs, out_specs=out_specs, check_vma=False)
```

profile of v0, /device:TPU:0, one launch (start us, length us, event | category | flops | bytes accessed | tf_op | source)
XLA Modules:
  0.0 303.1 jit_solution(3715893133542091083)
XLA Ops:
  6.5 0.0 all-gather.3.cloned.1.call-start
  6.5 0.7 all-gather.3.cloned.1.call-update
  7.3 0.0 all-gather.5.cloned.1.call-start
  7.3 0.7 convert_bitcast_fusion
  8.0 49.4 %all-gather.3.cloned.1.call-done = bf16[8192,384]{1,0:T(8,128)(2,1)} async-done(((bf16[1024,384]{1,0:T(8,128)(2,1)}), bf16[8192,384]{1,0:T(8,128)(2,1)}) %all-gather.3.cloned.1.call-update) | async-done | bytes 6291472 | tf_op jit(solution)/shard_map/all_gather | solution.py:29
  57.4 6.5 %mul.33 = bf16[8,128,64,128]{3,2,1,0:T(8,128)(2,1)} broadcast(bf16[8,64]{1,0:T(8,128)(2,1)S(1)} %convert_bitcast_fusion), dimensions={0,2} | broadcast | bytes 16778240 | tf_op jit(solution)/shard_map/mul | solution.py:25
  63.8 26.9 %fusion.7 = bf16[1024,384]{1,0:T(8,128)(2,1)} fusion(bf16[8192,384]{1,0:T(8,128)(2,1)} %all-gather.3.cloned.1.call-done, bf16[128,8,64,128]{3,2,1,0:T(8,128)(2,1)} %bitcast.25, bf16[1,1024,8192]{2,1,0:T(8,128)(2,1)} %param.4), kind=kOutput, calls=%fused_computation.15 | convolution fusion | flops 6451232768 | bytes 40632320 | tf_op jit(solution)/shard_map/dot_general | solution.py:27
  90.7 0.0 all-gather.5.cloned.1.call-update
  90.7 0.2 all-reduce.3.cloned.1.call-start
  90.9 0.0 copy-start.2
  91.0 63.1 %all-gather.5.cloned.1.call-done = bf16[1024,1536]{1,0:T(8,128)(2,1)} async-done(((bf16[1024,384]{1,0:T(8,128)(2,1)}), bf16[1024,1536]{1,0:T(8,128)(2,1)}) %all-gather.5.cloned.1.call-update) | async-done | bytes 3145744 | tf_op jit(solution)/shard_map/all_gather | solution.py:36
  154.1 0.0 copy-start
  154.1 5.2 %broadcast_select_fusion.1 = (bf16[1024,1536]{1,0:T(8,128)(2,1)}, bf16[1024,1536]{1,0:T(8,128)(2,1)}) fusion(bf16[1024,1536]{1,0:T(8,128)(2,1)} %all-gather.5.cloned.1.call-done, pred[]{:T(512)S(6)} %eq.6, pred[]{:T(512)S(6)} %eq.7), kind=kLoop, calls=%fused_computation.14 | loop fusion | flops 3145728 | bytes 9437186 | tf_op jit(solution)/shard_map/jit(_where)/select_n | solution.py:13
  159.3 0.0 all-reduce.3.cloned.1.call-update
  159.3 0.0 copy-done.2
  159.3 0.0 copy-done
  159.3 2.3 multiply_convert_fusion.1
  161.6 100.4 %all-reduce.3.cloned.1.call-done = (bf16[1024,1536]{1,0:T(8,128)(2,1)}, bf16[1024,1536]{1,0:T(8,128)(2,1)}) async-done(((bf16[1024,1536]{1,0:T(8,128)(2,1)}, bf16[1024,1536]{1,0:T(8,128)(2,1)}), (bf16[1024,1536]{1,0:T(8,128)(2,1)}, bf16[1024,1536]{1,0:T(8,128)(2,1)})) %all-reduce.3.cloned.1.call-update) | async-done | bytes 6291472 | tf_op jit(solution)/shard_map/psum | solution.py:14
  262.0 0.0 copy-start.1
  262.0 6.1 %pad_maximum_fusion = bf16[2048,1536]{1,0:T(8,128)(2,1)} fusion(bf16[1024,1536]{1,0:T(8,128)(2,1)} %get-tuple-element.5, bf16[1024,1536]{1,0:T(8,128)(2,1)} %get-tuple-element.6), kind=kLoop, calls=%fused_computation.9 | loop fusion | flops 12582912 | bytes 12582912 | tf_op jit(solution)/shard_map/concatenate | solution.py:43
  268.0 0.0 copy-done.1
  268.0 15.3 %convolution_convert_fusion = bf16[4,2048,1024]{2,1,0:T(8,128)(2,1)} fusion(bf16[256,4,8,384]{3,2,1,0:T(8,128)(2,1)} %bitcast.26, bf16[128,4,8,384]{3,2,1,0:T(8,128)(2,1)S(1)} %bitcast.27), kind=kOutput, calls=%fused_computation.5 | convolution fusion | flops 6450839552 | bytes 26214400 | tf_op jit(solution)/shard_map/ngk,mgk->gnm/dot_general | solution.py:47
  283.3 9.8 %convert_reduce_fusion = f32[2048,1024]{1,0:T(8,128)S(1)} fusion(bf16[4,2048,1024]{2,1,0:T(8,128)(2,1)} %convolution_convert_fusion), kind=kLoop, calls=%fused_computation | loop fusion | flops 14680064 | bytes 25165824 | tf_op jit(solution)/shard_map/reduce_sum | solution.py:49
  293.2 3.4 %multiply_convert_fusion = bf16[2048,1024]{1,0:T(8,128)(2,1)} fusion(f32[2048,1024]{1,0:T(8,128)S(1)} %convert_reduce_fusion), kind=kLoop, calls=%fused_computation.6 | loop fusion | flops 4194304 | bytes 12582912 | tf_op jit(solution)/shard_map/convert_element_type | solution.py:50
  (2 shorter events, 0.0 us)
Async XLA Ops:
  6.5 50.8 %all-gather.3.cloned.1.call-start = ((), (), s32[]{:S(2)}) async-start(), calls=%async_computation | async-start | bytes 7077888 | tf_op jit(solution)/shard_map/all_gather | solution.py:29
  7.3 146.8 %all-gather.5.cloned.1.call-start = ((), (), s32[]{:S(2)}) async-start(), calls=%async_computation.1 | async-start | bytes 3932160 | tf_op jit(solution)/shard_map/all_gather | solution.py:36
  90.7 171.3 %all-reduce.3.cloned.1.call-start = ((), (), s32[]{:S(2)}) async-start(), calls=%async_computation.2 | async-start | bytes 12582912 | tf_op jit(solution)/shard_map/psum | solution.py:14
  90.9 68.3 %copy-start.2 = (f32[384]{0:T(512)S(1)}, f32[384]{0:T(512)}, u32[]{:S(2)}) copy-start(f32[384]{0:T(512)} %param.7) | copy-start | bytes 4612
  154.1 5.2 %copy-start = (bf16[1024,1536]{1,0:T(8,128)(2,1)S(1)}, bf16[1024,1536]{1,0:T(8,128)(2,1)}, u32[]{:S(2)}) copy-start(bf16[1024,1536]{1,0:T(8,128)(2,1)} %all-gather.5.cloned.1.call-done) | copy-start | bytes 9437188
  262.0 6.1 %copy-start.1 = (bf16[1024,1536]{1,0:T(8,128)(2,1)S(1)}, bf16[1024,1536]{1,0:T(8,128)(2,1)}, u32[]{:S(2)}) copy-start(bf16[1024,1536]{1,0:T(8,128)(2,1)} %multiply_convert_fusion.1) | copy-start | bytes 9437188
Sparse Core Ops, SparseCore 0:
  9.2 48.1 all-gather.2
  90.8 63.2 all-gather.4
  159.4 102.5 all-reduce.2
where the time goes:
time: 303 us
  waiting for transfers between devices  214 us (71%)
  matrix products  42.1 us (14%)
  other arithmetic  27.4 us (9%)
  between operations  13.2 us (4%)
  local copies, waits for them, and re-layouts  6.49 us (2%)
    psum x1, waiting for transfers between devices, spread_2(): return lax.psum(block, axis)  100 us
    all_gather x1, waiting for transfers between devices, shards(): every = lax.all_gather(half, 'aux', axis=1, tiled=True)  63.1 us
    all_gather x1, waiting for transfers between devices, shards(): lax.all_gather(coefficients, 'bas', axis=0, tiled=True)  49.4 us
    dot_general x1, matrix products, shards(): jnp.dot(flat, lax.all_gather(coefficients, 'bas', axis=0, tiled=True), pr...  26.9 us
    dot_general x1, matrix products, shards(): jnp.einsum('ngk,mgk->gnm', left, right, preferred_element_type=jnp.float32)  15.3 us
    reduce_sum x1, other arithmetic, shards(): total = jnp.sum(rounded.astype(jnp.float32), axis=0)  9.83 us
    mul x1, local copies, waits for them, and re-layouts, shards(): integrals.reshape(aux_count, row_blocks, BLOCK, col_blocks, BLOCK) * masks  6.46 us
  transfers between devices with their start and end apart: 3, of which 3 were waited for; matrix products, arithmetic and copies ran while one was open for 1% of the time, Pallas kernels for 0%

commit v1 on v0

--- a/solution.py
+++ b/solution.py
@@ -7,6 +7,18 @@
 NOCC = 384
 BLOCK = 128
 AUX_DEV = 1
+
+
+def register_the_bars(u, which_axis):
+    shares = lax.axis_size(which_axis)
+    e_next = [(ii - 1, ii) for ii in range(1, shares)] + [(shares - 1, 0)]
+    x_new = u
+    pieces_in = [x_new]
+    for _ in tuple(range(shares - 1)):
+        x_new = lax.ppermute(x_new, which_axis, e_next)
+        pieces_in += [x_new]
+    y1 = jnp.concatenate([*reversed(pieces_in)], axis=1)
+    return jnp.roll(y1, (lax.axis_index(which_axis) + 1) * x_new.shape[1], axis=1)
 
 
 def spread_2(block, axis, owner):
@@ -33,7 +45,7 @@
     half = half.reshape(row_count, aux_count * occ_count).astype(jnp.bfloat16)
     aux_groups = lax.axis_size("aux")
     scale = 1.0 / math.sqrt(AUX_DEV * aux_groups * NOCC)
-    every = lax.all_gather(half, "aux", axis=1, tiled=True)
+    every = register_the_bars(half, "aux")
     weighted_all = (every.astype(jnp.float32) * jnp.tile(weights, aux_count * aux_groups)).astype(
         jnp.bfloat16
     )

time: 303 us -> 287 us (0.947)
  matrix products: 42.1 us -> 28.2 us
  waiting for transfers between devices: 214 us -> 207 us
  local copies, waits for them, and re-layouts: 6.49 us -> 10.3 us
    all_gather x1 -> x0, waiting for transfers between devices: 63.1 us -> none  [shards(): every = lax.all_gather(half, 'aux', axis=1, tiled=True)]
    ppermute x0 -> x3, waiting for transfers between devices: none -> 60.4 us  [register_the_bars(): x_new = lax.ppermute(x_new, which_axis, e_next)]
    dot_general x1, matrix products: 26.9 us -> 13.9 us  [shards(): jnp.dot(flat, lax.all_gather(coefficients, 'bas', axis=0, tiled=True), pr...]
    psum x1, waiting for transfers between devices: 100 us -> 96.8 us  [spread_2(): return lax.psum(block, axis)]
  transfers between devices with their start and end apart: 3 -> 5, of which waited for: 3 -> 5; matrix products, arithmetic and copies ran while one was open for 1% -> 2% of each run, Pallas kernels for 0% -> 0%
where the time goes in v1:
time: 287 us
  waiting for transfers between devices  207 us (72%)
  matrix products  28.2 us (10%)
  other arithmetic  26 us (9%)
  between operations  13.5 us (5%)
  local copies, waits for them, and re-layouts  10.3 us (4%)
    psum x1, waiting for transfers between devices, spread_2(): return lax.psum(block, axis)  96.8 us
    ppermute x3, waiting for transfers between devices, register_the_bars(): x_new = lax.ppermute(x_new, which_axis, e_next)  60.4 us
    all_gather x1, waiting for transfers between devices, shards(): lax.all_gather(coefficients, 'bas', axis=0, tiled=True)  49.4 us
    dot_general x1, matrix products, shards(): jnp.einsum('ngk,mgk->gnm', left, right, preferred_element_type=jnp.float32)  14.3 us
    dot_general x1, matrix products, shards(): jnp.dot(flat, lax.all_gather(coefficients, 'bas', axis=0, tiled=True), pr...  13.9 us
    reduce_sum x1, other arithmetic, shards(): total = jnp.sum(rounded.astype(jnp.float32), axis=0)  9.83 us
    mul x1, local copies, waits for them, and re-layouts, shards(): integrals.reshape(aux_count, row_blocks, BLOCK, col_blocks, BLOCK) * masks  7.25 us
  transfers between devices with their start and end apart: 5, of which 5 were waited for; matrix products, arithmetic and copies ran while one was open for 2% of the time, Pallas kernels for 0%

profile of v1, /device:TPU:0, one launch (start us, length us, event | category | flops | bytes accessed | tf_op | source)
XLA Modules:
  0.0 287.0 jit_solution(6781122564902658973)
XLA Ops:
  6.5 0.0 all-gather.2.cloned.1.call-start
  6.5 0.7 all-gather.2.cloned.1.call-update
  7.3 0.0 all-reduce.3.cloned.1.call-start
  7.3 0.7 convert_bitcast_fusion
  8.0 49.4 %all-gather.2.cloned.1.call-done = bf16[8192,384]{1,0:T(8,128)(2,1)} async-done(((bf16[1024,384]{1,0:T(8,128)(2,1)}), bf16[8192,384]{1,0:T(8,128)(2,1)}) %all-gather.2.cloned.1.call-update) | async-done | bytes 6291472 | tf_op jit(solution)/shard_map/all_gather | solution.py:41
  57.4 0.0 copy-start.2
  57.4 7.2 %mul.36 = bf16[8,128,64,128]{3,2,1,0:T(8,128)(2,1)} broadcast(bf16[8,64]{1,0:T(8,128)(2,1)S(1)} %convert_bitcast_fusion), dimensions={0,2} | broadcast | bytes 16778240 | tf_op jit(solution)/shard_map/mul | solution.py:37
  64.6 0.0 copy-done.2
  64.6 13.9 %fusion.3 = bf16[1024,384]{0,1:T(8,128)(2,1)S(1)} fusion(bf16[8192,384]{1,0:T(8,128)(2,1)S(1)} %copy-done.2, bf16[128,8,64,128]{3,2,1,0:T(8,128)(2,1)} %bitcast.21, bf16[1,1024,8192]{2,1,0:T(8,128)(2,1)} %param.4), kind=kOutput, calls=%fused_computation.11 | convolution fusion | flops 6451232768 | bytes 40632320 | tf_op jit(solution)/shard_map/dot_general | solution.py:39
  78.6 1.5 collective-permute-start
  80.1 20.0 %collective-permute-done = bf16[1024,384]{0,1:T(8,128)(2,1)S(1)} collective-permute-done((bf16[1024,384]{0,1:T(8,128)(2,1)S(1)}, bf16[1024,384]{0,1:T(8,128)(2,1)S(1)}, u32[]{:S(2)}, u32[]{:S(2)}) %collective-permute-start) | collective-permute-done | bytes 786464 | tf_op jit(solution)/shard_map/ppermute | solution.py:18
  100.1 0.0 collective-permute-start.1
  100.1 20.6 %collective-permute-done.1 = bf16[1024,384]{0,1:T(8,128)(2,1)S(1)} collective-permute-done((bf16[1024,384]{0,1:T(8,128)(2,1)S(1)}, bf16[1024,384]{0,1:T(8,128)(2,1)S(1)}, u32[]{:S(2)}, u32[]{:S(2)}) %collective-permute-start.1) | collective-permute-done | bytes 786464 | tf_op jit(solution)/shard_map/ppermute | solution.py:18
  120.7 0.0 collective-permute-start.2
  120.7 19.8 %collective-permute-done.2 = bf16[1024,384]{0,1:T(8,128)(2,1)S(1)} collective-permute-done((bf16[1024,384]{0,1:T(8,128)(2,1)S(1)}, bf16[1024,384]{0,1:T(8,128)(2,1)S(1)}, u32[]{:S(2)}, u32[]{:S(2)}) %collective-permute-start.2) | collective-permute-done | bytes 786464 | tf_op jit(solution)/shard_map/ppermute | solution.py:18
  140.5 0.1 constant_dynamic-update-slice_fusion.7
  140.6 0.1 constant_dynamic-update-slice_fusion.6
  140.6 0.1 constant_dynamic-update-slice_fusion.5
  140.7 0.1 constant_dynamic-update-slice_fusion.4
  140.7 0.1 constant_dynamic-update-slice_fusion.3
  140.8 0.1 constant_dynamic-update-slice_fusion.2
  140.9 0.1 constant_dynamic-update-slice_fusion.1
  140.9 0.1 constant_dynamic-update-slice_fusion
  141.0 0.0 copy-start
  141.0 2.7 copy-done
  143.7 0.0 copy-start.1
  143.7 4.2 %broadcast_select_fusion.1 = (bf16[1024,1536]{0,1:T(8,128)(2,1)}, bf16[1024,1536]{0,1:T(8,128)(2,1)}) fusion(pred[]{:T(512)S(6)} %eq.9, bf16[1024,3072]{0,1:T(8,128)(2,1)S(1)} %constant_dynamic-update-slice_fusion, s32[]{:T(128)S(6)} %select_n.29, pred[]{:T(512)S(6)} %eq.10), kind=kLoop, calls=%fused_computation.10 | loop fusion | flops 3145728 | bytes 9437190 | tf_op jit(solution)/shard_map/jit(_where)/select_n | solution.py:25
  147.8 0.0 all-reduce.3.cloned.1.call-update
  147.8 0.0 copy-done.1
  147.9 4.5 %multiply_convert_fusion.1 = bf16[1024,1536]{0,1:T(8,128)(2,1)} fusion(f32[1536]{0:T(1024)S(1)} %mul.40, bf16[1024,3072]{0,1:T(8,128)(2,1)} %copy-done, s32[]{:T(128)S(6)} %select_n.29), kind=kLoop, calls=%fused_computation.8 | loop fusion | flops 4718592 | bytes 6297604 | tf_op jit(solution)/shard_map/convert_element_type | solution.py:49
  152.4 96.8 %all-reduce.3.cloned.1.call-done = (bf16[1024,1536]{0,1:T(8,128)(2,1)}, bf16[1024,1536]{0,1:T(8,128)(2,1)}) async-done(((bf16[1024,1536]{0,1:T(8,128)(2,1)}, bf16[1024,1536]{0,1:T(8,128)(2,1)}), (bf16[1024,1536]{0,1:T(8,128)(2,1)}, bf16[1024,1536]{0,1:T(8,128)(2,1)})) %all-reduce.3.cloned.1.call-update) | async-done | bytes 6291472 | tf_op jit(solution)/shard_map/psum | solution.py:26
  249.2 3.4 %pad_maximum_fusion = bf16[2048,1536]{0,1:T(8,128)(2,1)S(1)} fusion(bf16[1024,1536]{0,1:T(8,128)(2,1)} %get-tuple-element.5, bf16[1024,1536]{0,1:T(8,128)(2,1)} %get-tuple-element.6), kind=kLoop, calls=%fused_computation.7 | loop fusion | flops 12582912 | bytes 12582912 | tf_op jit(solution)/shard_map/concatenate | solution.py:55
  252.6 14.3 %convolution_convert_fusion = bf16[4,2048,1024]{2,1,0:T(8,128)(2,1)} fusion(bf16[2048,4,384]{0,2,1:T(8,128)(2,1)S(1)} %bitcast.22, bf16[1024,4,384]{0,2,1:T(8,128)(2,1)} %bitcast.23), kind=kOutput, calls=%fused_computation.5 | convolution fusion | flops 6450839552 | bytes 26214400 | tf_op jit(solution)/shard_map/ngk,mgk->gnm/dot_general | solution.py:59
  266.9 9.8 %convert_reduce_fusion = f32[2048,1024]{1,0:T(8,128)S(1)} fusion(bf16[4,2048,1024]{2,1,0:T(8,128)(2,1)} %convolution_convert_fusion), kind=kLoop, calls=%fused_computation | loop fusion | flops 14680064 | bytes 25165824 | tf_op jit(solution)/shard_map/reduce_sum | solution.py:61
  276.8 3.4 %multiply_convert_fusion = bf16[2048,1024]{1,0:T(8,128)(2,1)} fusion(f32[2048,1024]{1,0:T(8,128)S(1)} %convert_reduce_fusion), kind=kLoop, calls=%fused_computation.6 | loop fusion | flops 4194304 | bytes 12582912 | tf_op jit(solution)/shard_map/convert_element_type | solution.py:62
  (2 shorter events, 0.0 us)
Async XLA Ops:
  6.5 50.8 %all-gather.2.cloned.1.call-start = ((), (), s32[]{:S(2)}) async-start(), calls=%async_computation | async-start | bytes 7077888 | tf_op jit(solution)/shard_map/all_gather | solution.py:41
  7.3 241.9 %all-reduce.3.cloned.1.call-start = ((), (), s32[]{:S(2)}) async-start(), calls=%async_computation.1 | async-start | bytes 12582912 | tf_op jit(solution)/shard_map/psum | solution.py:26
  57.4 7.3 %copy-start.2 = (bf16[8192,384]{1,0:T(8,128)(2,1)S(1)}, bf16[8192,384]{1,0:T(8,128)(2,1)}, u32[]{:S(2)}) copy-start(bf16[8192,384]{1,0:T(8,128)(2,1)} %all-gather.2.cloned.1.call-done) | copy-start | bytes 18874372
  78.6 21.5 %collective-permute-start = (bf16[1024,384]{0,1:T(8,128)(2,1)S(1)}, bf16[1024,384]{0,1:T(8,128)(2,1)S(1)}, u32[]{:S(2)}, u32[]{:S(2)}) collective-permute-start(bf16[1024,384]{0,1:T(8,128)(2,1)S(1)} %fusion.3), channel_id=1, source_target_pairs={{0,1},{1,2},{2,3},{3,0},{4,5},{5,6},{6,7},{7,4},{8,9},{9,10},{10,1... | collective-permute-start | bytes 2359304 | tf_op jit(solution)/shard_map/ppermute | solution.py:18
  100.1 20.6 %collective-permute-start.1 = (bf16[1024,384]{0,1:T(8,128)(2,1)S(1)}, bf16[1024,384]{0,1:T(8,128)(2,1)S(1)}, u32[]{:S(2)}, u32[]{:S(2)}) collective-permute-start(bf16[1024,384]{0,1:T(8,128)(2,1)S(1)} %collective-permute-done), channel_id=1, source_target_pairs={{0,1},{1,2},{2,3},{3,0},{4,5},{5,6},{6,7},{7,4},{8,9},{9,10},{10,1... | collective-permute-start | bytes 2359304 | tf_op jit(solution)/shard_map/ppermute | solution.py:18
  120.7 19.8 %collective-permute-start.2 = (bf16[1024,384]{0,1:T(8,128)(2,1)S(1)}, bf16[1024,384]{0,1:T(8,128)(2,1)S(1)}, u32[]{:S(2)}, u32[]{:S(2)}) collective-permute-start(bf16[1024,384]{0,1:T(8,128)(2,1)S(1)} %collective-permute-done.1), channel_id=1, source_target_pairs={{0,1},{1,2},{2,3},{3,0},{4,5},{5,6},{6,7},{7,4},{8,9},{9,10},{10,1... | collective-permute-start | bytes 2359304 | tf_op jit(solution)/shard_map/ppermute | solution.py:18
  141.0 2.7 copy-start
  143.7 4.2 %copy-start.1 = (f32[384]{0:T(512)S(1)}, f32[384]{0:T(512)}, u32[]{:S(2)}) copy-start(f32[384]{0:T(512)} %param.7) | copy-start | bytes 4612
Sparse Core Ops, SparseCore 0:
  9.2 48.1 all-gather.1
  148.0 101.1 all-reduce.2
